TPU v7x, 512 devices: a whole 4x4x16 slice. The times are simulated.
512 devices in a mesh: grp: 16 (over z), cube: 32 (over y, x, core).
Axes of the slice: x: 4, y: 4, z: 16, core: 2. Of those that a mesh axis runs over, the one named last changes fastest.
Arguments:
- density: float32 [16, 32, 64, 512], P('grp', 'cube'), may hold values from 0.5 to 2
- momentum: float32 [16, 32, 3, 64, 512], P('grp', 'cube'), may hold values from -3 to 3
- element_size: float32 [16, 32, 3, 64], P('grp', 'cube'), may hold values from 0.5 to 2
- section_slots: int32 [16, 32, 5, 1024], P('grp', 'cube'), may hold values from 0 to 28671, as said below
- section_counts: int32 [16, 32, 5], P('grp', 'cube'), may hold values from 512 to 1024, as said below
- cross_slots: int32 [16, 32, 2, 1024], P('grp', 'cube'), may hold values from 0 to 28671, as said below
- cross_counts: int32 [16, 32, 2], P('grp', 'cube'), may hold values from 512 to 1024, as said below
Outputs:
- new_density: float32 [16, 32, 64, 512], P('grp', 'cube')
- new_momentum: float32 [16, 32, 3, 64, 512], P('grp', 'cube')
Inputs may be any that keep to these rules, and one draw needn't show every extreme that they name: All slots of a device, of section_slots and cross_slots together, name different nodes. `section_counts`: the two devices of a pair have the same count for that bit; some pair fills all 1024 slots. All slots of a device, of section_slots and cross_slots together, name different nodes. `cross_counts`: a device's count toward the upper group equals the upper device's count toward the lower group; some pair fills all 1024 slots.
All inputs are finite; a program needn't handle non-finite values.
Results may differ from a plain program's by a relative error of at most 0.0003.
Values sent between devices are 32-bit elements; how exact they have to be, the bound alone decides.
No kernel may reach another device: no remote copies, remote signals or barrier semaphores. Data moves between devices by JAX's collectives and lax.ppermute only.
A program may use at most 64 MiB of HBM per device.

v0:
```python
import jax
import jax.numpy as jnp
import numpy as np
from jax import lax
from jax.sharding import PartitionSpec as P

GAMMA = 1.4
DT = 0.01
ORDER = 7


def with_halo(cells, sides, width):
    for axis, dim in sides:
        count = lax.axis_size(axis)
        head = lax.slice_in_dim(cells, 0, width, axis=dim)
        tail = lax.slice_in_dim(cells, cells.shape[dim] - width, cells.shape[dim], axis=dim)
        cells = jnp.concatenate(
            [
                lax.ppermute(tail, axis, [(i, (i + 1) % count) for i in range(count)]),
                cells,
                lax.ppermute(head, axis, [((i + 1) % count, i) for i in range(count)]),
            ],
            axis=dim,
        )
    return cells


def gll_tables():
    points = np.array(
        [
            -1.0,
            -0.8717401485096066,
            -0.5917001814331423,
            -0.2092992179024789,
            0.2092992179024789,
            0.5917001814331423,
            0.8717401485096066,
            1.0,
        ]
    )
    weights = np.array(
        [
            1.0 / 28.0,
            0.2107042271435061,
            0.3411226924835044,
            0.4124587946587038,
            0.4124587946587038,
            0.3411226924835044,
            0.2107042271435061,
            1.0 / 28.0,
        ]
    )
    previous = np.ones(8)
    current = points.copy()
    for order_now in range(1, ORDER):
        following = ((2 * order_now + 1) * points * current - order_now * previous) / (
            order_now + 1
        )
        previous = current
        current = following
    derivative = np.zeros((8, 8))
    for i in range(8):
        for j in range(8):
            if i != j:
                derivative[i, j] = current[i] / (current[j] * (points[i] - points[j]))
    derivative[0, 0] = -ORDER * (ORDER + 1) / 4.0
    derivative[7, 7] = ORDER * (ORDER + 1) / 4.0
    return (points, weights, derivative)


def derivative_tables():
    points, weights, derivative = gll_tables()
    eye_eight = np.eye(8)
    eye_wide = np.eye(64)
    along_first = np.kron(derivative, eye_wide)
    along_second = np.kron(eye_eight, np.kron(derivative, eye_eight))
    along_third = np.kron(eye_wide, derivative)
    tables = [jnp.asarray(t.T, jnp.float32) for t in (along_first, along_second, along_third)]
    node_weight = jnp.asarray(np.kron(weights, np.kron(weights, weights)), jnp.float32)
    return (tables, node_weight)


def split_onehots(row_ids, high_count):
    high_part = (row_ids[:, None] // 128 == jnp.arange(high_count, dtype=jnp.int32)[None]).astype(
        jnp.float32
    )
    low_part = (row_ids[:, None] % 128 == jnp.arange(128, dtype=jnp.int32)[None]).astype(
        jnp.float32
    )
    return (high_part, low_part)


def pick_rows(table, slot_ids, counts):
    high_count = table.shape[0]
    flat_table = table.reshape(high_count, 640)

    def pick_one_row(pieces):
        row_ids, count = pieces
        high_part, low_part = split_onehots(row_ids, high_count)
        rows_high = jnp.dot(high_part, flat_table, precision=lax.Precision.HIGHEST).reshape(
            -1, 5, 128
        )
        picked = jnp.sum(rows_high * low_part[:, None, :], axis=2)
        live_mask = (jnp.arange(row_ids.shape[0]) < count).astype(jnp.float32)
        return (picked * live_mask[:, None]).T

    return jnp.moveaxis(lax.map(pick_one_row, (slot_ids, counts)), 0, 1)


def add_rows(table, slot_ids, incoming):
    high_count = table.shape[0]

    def add_one_row(carry, pieces):
        row_ids, values = pieces
        high_part, low_part = split_onehots(row_ids, high_count)
        spread = (values.T[:, :, None] * low_part[:, None, :]).reshape(-1, 640)
        added = lax.dot_general(
            high_part, spread, (((0,), (0,)), ((), ())), precision=lax.Precision.HIGHEST
        )
        return (carry + added, None)

    flat_table, unused = lax.scan(
        add_one_row, table.reshape(high_count, 640), (slot_ids, jnp.moveaxis(incoming, 1, 0))
    )
    return flat_table.reshape(high_count, 5, 128)


def local(
    density, momentum, element_size, section_slots, section_counts, cross_slots, cross_counts
):
    mass_density = density[0, 0]
    moment = momentum[0, 0]
    extents = element_size[0, 0]
    elements = mass_density.shape[0]
    distinct = 7 * 64 * elements
    high_count = distinct // 128
    tables, node_weight = derivative_tables()
    velocity = moment / mass_density[None]
    pressure = jnp.exp(GAMMA * jnp.log(mass_density))
    scales = 2.0 / extents
    residual = jnp.zeros((4, elements, 512), jnp.float32)
    for axis_num in range(3):
        mom_flux = moment * velocity[axis_num][None]
        mom_flux = mom_flux.at[axis_num].add(pressure)
        fluxes = (
            jnp.concatenate([moment[axis_num][None], mom_flux], axis=0)
            * scales[axis_num][None, :, None]
        )
        change = jnp.dot(
            fluxes.reshape(4 * elements, 512), tables[axis_num], precision=lax.Precision.HIGHEST
        )
        residual = residual - change.reshape(4, elements, 512)
    jacobian = extents[0] * extents[1] * extents[2] / 8.0
    weight = jacobian[:, None] * node_weight[None]
    values = jnp.concatenate([residual * weight[None], weight[None]], axis=0).reshape(
        5, elements, 8, 64
    )
    last_face = jnp.roll(values[:, :, 7], 1, axis=1)
    first_face = values[:, :, 0] + last_face
    slabs = jnp.concatenate([first_face[:, :, None], values[:, :, 1:7]], axis=2)
    sums = slabs.reshape(5, high_count, 128)
    table = jnp.moveaxis(sums, 0, 1)
    section_ids = section_slots[0, 0]
    cross_ids = cross_slots[0, 0]
    section_send = pick_rows(table, section_ids, section_counts[0, 0])
    cross_send = pick_rows(table, cross_ids, cross_counts[0, 0])
    sections = lax.axis_size("cube").bit_length() - 1
    received = []
    gathered = lax.all_gather(section_send[None], "cube", axis=0, tiled=True)
    position = lax.axis_index("cube")
    for b in range(sections):
        partner = jnp.bitwise_xor(position, 1 << b)
        partner_block = lax.dynamic_index_in_dim(gathered, partner, 0, keepdims=False)
        received.append(partner_block[:, b])
    section_recv = jnp.stack(received, axis=1)
    padded = with_halo(cross_send, (("grp", 1),), 1)
    cross_recv = jnp.stack([padded[:, 0], padded[:, 3]], axis=1)
    table = add_rows(table, section_ids, section_recv)
    table = add_rows(table, cross_ids, cross_recv)
    totals = jnp.moveaxis(table, 0, 1)
    assembled = (totals[:4] / totals[4:]).reshape(4, elements, 7, 64)
    next_face = jnp.roll(assembled[:, :, 0], -1, axis=1)
    at_nodes = jnp.concatenate([assembled, next_face[:, :, None]], axis=2).reshape(4, elements, 512)
    new_density = mass_density + DT * at_nodes[0]
    new_momentum = moment + DT * at_nodes[1:]
    return (new_density[None, None], new_momentum[None, None])


def solution(mesh):
    placed = (
        P("grp", "cube", None, None),
        P("grp", "cube", None, None, None),
        P("grp", "cube", None, None),
        P("grp", "cube", None, None),
        P("grp", "cube", None),
        P("grp", "cube", None, None),
        P("grp", "cube", None),
    )
    return jax.shard_map(
        local,
        mesh=mesh,
        in_specs=placed,
        out_specs=(P("grp", "cube", None, None), P("grp", "cube", None, None, None)),
        check_vma=False,
    )
```

profile of v0, /device:TPU:1, one launch (start us, length us, event | category | flops | bytes accessed | tf_op | source)
XLA Modules:
  0.0 140.9 jit_solution(12547658558142981243)
XLA Ops:
  8.7 1.1 slice_bitcast_fusion.5
  9.8 1.1 bitcast_divide_fusion
  12.1 1.1 convolution_subtract_fusion.2
  13.2 1.1 convolution_subtract_fusion.1
  14.3 1.1 fusion.25
  17.2 24.8 %while.51 = (s32[]{:T(128)}, f32[5,5,1024]{2,0,1:T(8,128)}, s32[5,1024]{1,0:T(8,128)S(1)}, f32[224,640]{1,0:T(8,128)S(1)}, s32[5]{0:T(128)S(1)}, /*index=5*/s32[]{:T(128)}, s32[]{:T(128)}) while((s32[]{:T(128)}, f32[5,5,1024]{2,0,1:T(8,128)}, s32[5,1024]{1,0:T(8,128)S(1)}, f32[224,640]{1,0:T(8,128)S(1)}, s32[5]{0:T(128)S(1)}, ...), condition=%wide.region_2.0_spmd, body=%wide.region_0.2_spmd.sunk | while | flops 1763431424 | bytes 7045221 | solution.py:107
  17.2 1.4 %fusion.65 = f32[1024,640]{0,1:T(8,128)S(1)} fusion(f32[224,640]{1,0:T(8,128)S(1)} %get-tuple-element.535, s32[1024]{0:T(1024)S(1)} %get-tuple-element.497), kind=kOutput, calls=%fused_computation.2.clone.1 | convolution fusion | flops 1761837056 | bytes 3198976 | tf_op jit(solution)/shard_map/while/body/eval_jaxpr/dot_general | solution.py:100
  20.5 1.7 %dynamic_update_slice.17 = f32[5,5,1024]{2,0,1:T(8,128)} dynamic-update-slice(f32[5,5,1024]{2,0,1:T(8,128)} %get-tuple-element.526, f32[1,5,1024]{2,0,1:T(1,128)S(1)} %copy.62, s32[]{:T(128)} %get-tuple-element.525, s32[]{:T(128)} %constant.335.clone.1..sunk, s32[]{:T(128)} %constant.335.clone.1..sunk) | dynamic-update-slice | bytes 40964 | tf_op jit(solution)/shard_map/while/body/jit(dynamic_update_index_in_dim)/dynamic_update_slice | solution.py:107
  22.2 1.5 %fusion.65 = f32[1024,640]{0,1:T(8,128)S(1)} fusion(f32[224,640]{1,0:T(8,128)S(1)} %get-tuple-element.535, s32[1024]{0:T(1024)S(1)} %get-tuple-element.497), kind=kOutput, calls=%fused_computation.2.clone.1 | convolution fusion | flops 1761837056 | bytes 3198976 | tf_op jit(solution)/shard_map/while/body/eval_jaxpr/dot_general | solution.py:100
  25.5 1.7 %dynamic_update_slice.17 = f32[5,5,1024]{2,0,1:T(8,128)} dynamic-update-slice(f32[5,5,1024]{2,0,1:T(8,128)} %get-tuple-element.526, f32[1,5,1024]{2,0,1:T(1,128)S(1)} %copy.62, s32[]{:T(128)} %get-tuple-element.525, s32[]{:T(128)} %constant.335.clone.1..sunk, s32[]{:T(128)} %constant.335.clone.1..sunk) | dynamic-update-slice | bytes 40964 | tf_op jit(solution)/shard_map/while/body/jit(dynamic_update_index_in_dim)/dynamic_update_slice | solution.py:107
  27.1 1.4 %fusion.65 = f32[1024,640]{0,1:T(8,128)S(1)} fusion(f32[224,640]{1,0:T(8,128)S(1)} %get-tuple-element.535, s32[1024]{0:T(1024)S(1)} %get-tuple-element.497), kind=kOutput, calls=%fused_computation.2.clone.1 | convolution fusion | flops 1761837056 | bytes 3198976 | tf_op jit(solution)/shard_map/while/body/eval_jaxpr/dot_general | solution.py:100
  30.4 1.7 %dynamic_update_slice.17 = f32[5,5,1024]{2,0,1:T(8,128)} dynamic-update-slice(f32[5,5,1024]{2,0,1:T(8,128)} %get-tuple-element.526, f32[1,5,1024]{2,0,1:T(1,128)S(1)} %copy.62, s32[]{:T(128)} %get-tuple-element.525, s32[]{:T(128)} %constant.335.clone.1..sunk, s32[]{:T(128)} %constant.335.clone.1..sunk) | dynamic-update-slice | bytes 40964 | tf_op jit(solution)/shard_map/while/body/jit(dynamic_update_index_in_dim)/dynamic_update_slice | solution.py:107
  32.1 1.5 %fusion.65 = f32[1024,640]{0,1:T(8,128)S(1)} fusion(f32[224,640]{1,0:T(8,128)S(1)} %get-tuple-element.535, s32[1024]{0:T(1024)S(1)} %get-tuple-element.497), kind=kOutput, calls=%fused_computation.2.clone.1 | convolution fusion | flops 1761837056 | bytes 3198976 | tf_op jit(solution)/shard_map/while/body/eval_jaxpr/dot_general | solution.py:100
  35.4 1.7 %dynamic_update_slice.17 = f32[5,5,1024]{2,0,1:T(8,128)} dynamic-update-slice(f32[5,5,1024]{2,0,1:T(8,128)} %get-tuple-element.526, f32[1,5,1024]{2,0,1:T(1,128)S(1)} %copy.62, s32[]{:T(128)} %get-tuple-element.525, s32[]{:T(128)} %constant.335.clone.1..sunk, s32[]{:T(128)} %constant.335.clone.1..sunk) | dynamic-update-slice | bytes 40964 | tf_op jit(solution)/shard_map/while/body/jit(dynamic_update_index_in_dim)/dynamic_update_slice | solution.py:107
  37.1 1.4 %fusion.65 = f32[1024,640]{0,1:T(8,128)S(1)} fusion(f32[224,640]{1,0:T(8,128)S(1)} %get-tuple-element.535, s32[1024]{0:T(1024)S(1)} %get-tuple-element.497), kind=kOutput, calls=%fused_computation.2.clone.1 | convolution fusion | flops 1761837056 | bytes 3198976 | tf_op jit(solution)/shard_map/while/body/eval_jaxpr/dot_general | solution.py:100
  40.3 1.7 %dynamic_update_slice.17 = f32[5,5,1024]{2,0,1:T(8,128)} dynamic-update-slice(f32[5,5,1024]{2,0,1:T(8,128)} %get-tuple-element.526, f32[1,5,1024]{2,0,1:T(1,128)S(1)} %copy.62, s32[]{:T(128)} %get-tuple-element.525, s32[]{:T(128)} %constant.335.clone.1..sunk, s32[]{:T(128)} %constant.335.clone.1..sunk) | dynamic-update-slice | bytes 40964 | tf_op jit(solution)/shard_map/while/body/jit(dynamic_update_index_in_dim)/dynamic_update_slice | solution.py:107
  42.0 6.4 %while.53 = (s32[]{:T(128)}, f32[2,5,1024]{2,1,0:T(8,128)S(1)}, s32[2,1024]{1,0:T(2,128)S(1)}, f32[224,640]{1,0:T(8,128)S(1)}, s32[2]{0:T(128)S(1)}, /*index=5*/s32[]{:T(128)}) while((s32[]{:T(128)}, f32[2,5,1024]{2,1,0:T(8,128)S(1)}, s32[2,1024]{1,0:T(2,128)S(1)}, f32[224,640]{1,0:T(8,128)S(1)}, s32[2]{0:T(128)S(1)}, ...), condition=%wide.region_7.8_spmd, body=%wide.region_5.7_spmd.sunk | while | flops 1763431424 | bytes 6987869 | solution.py:107
  42.1 1.5 %fusion.72 = f32[1024,640]{0,1:T(8,128)S(1)} fusion(f32[224,640]{1,0:T(8,128)S(1)} %get-tuple-element.569, s32[1024]{0:T(1024)S(1)} %get-tuple-element.510), kind=kOutput, calls=%fused_computation.37.clone.1 | convolution fusion | flops 1761837056 | bytes 3198976 | tf_op jit(solution)/shard_map/while/body/eval_jaxpr/dot_general | solution.py:100
  45.3 1.4 %fusion.72 = f32[1024,640]{0,1:T(8,128)S(1)} fusion(f32[224,640]{1,0:T(8,128)S(1)} %get-tuple-element.569, s32[1024]{0:T(1024)S(1)} %get-tuple-element.510), kind=kOutput, calls=%fused_computation.37.clone.1 | convolution fusion | flops 1761837056 | bytes 3198976 | tf_op jit(solution)/shard_map/while/body/eval_jaxpr/dot_general | solution.py:100
  48.4 4.4 %collective-permute-start = (f32[5,1,1024]{2,0,1:T(8,128)S(1)}, f32[5,1,1024]{2,0,1:T(8,128)S(1)}, u32[]{:S(2)}, u32[]{:S(2)}) collective-permute-start(f32[5,1,1024]{2,0,1:T(8,128)S(1)} %get-tuple-element.381), channel_id=1, source_target_pairs={{0,32},{32,64},{64,96},{96,128},{128,160},{160,192},{192,224},{224... | collective-permute-start | bytes 61448 | tf_op jit(solution)/shard_map/ppermute | solution.py:19
  52.8 9.7 %collective-permute-start.1 = (f32[5,1,1024]{2,0,1:T(8,128)S(1)}, f32[5,1,1024]{2,0,1:T(8,128)S(1)}, u32[]{:S(2)}, u32[]{:S(2)}) collective-permute-start(f32[5,1,1024]{2,0,1:T(8,128)S(1)} %get-tuple-element.382), channel_id=1, source_target_pairs={{32,0},{64,32},{96,64},{128,96},{160,128},{192,160},{224,192},{256... | collective-permute-start | bytes 61448 | tf_op jit(solution)/shard_map/ppermute | solution.py:21
  63.3 47.1 %all-gather.3.cloned.1.call-done = f32[160,5,1024]{2,1,0:T(8,128)} async-done(((f32[5,5,1024]{2,1,0:T(8,128)}), f32[160,5,1024]{2,1,0:T(8,128)}) %all-gather.3.cloned.1.call-update) | async-done | bytes 3276816 | tf_op jit(solution)/shard_map/all_gather | solution.py:169
  110.4 1.3 constant_dynamic-slice_fusion.4
  112.2 13.4 %while.52 = (s32[]{:T(128)}, f32[224,640]{1,0:T(8,128)S(1)}, s32[5,1024]{1,0:T(8,128)S(1)}, f32[5,5,1024]{2,1,0:T(8,128)S(1)}, s32[]{:T(128)}) while((s32[]{:T(128)}, f32[224,640]{1,0:T(8,128)S(1)}, s32[5,1024]{1,0:T(8,128)S(1)}, f32[5,5,1024]{2,1,0:T(8,128)S(1)}, s32[]{:T(128)}) %tuple.161), condition=%wide.region_4.5_spmd, body=%wide.region_3.4_spmd.sunk | while | flops 1763146752 | bytes 7528517 | solution.py:122
  112.6 2.2 %convolution_add_fusion.4 = f32[224,640]{1,0:T(8,128)S(1)} fusion(f32[224,640]{1,0:T(8,128)S(1)} %get-tuple-element.545, f32[1024,640]{0,1:T(8,128)S(1)} %bitcast.147, s32[1024]{0:T(1024)S(1)} %get-tuple-element.504), kind=kOutput, calls=%fused_computation.19.clone.1 | convolution fusion | flops 1762209792 | bytes 3772416 | tf_op jit(solution)/shard_map/while/body/eval_jaxpr/dot_general | solution.py:117
  115.3 2.2 %convolution_add_fusion.4 = f32[224,640]{1,0:T(8,128)S(1)} fusion(f32[224,640]{1,0:T(8,128)S(1)} %get-tuple-element.545, f32[1024,640]{0,1:T(8,128)S(1)} %bitcast.147, s32[1024]{0:T(1024)S(1)} %get-tuple-element.504), kind=kOutput, calls=%fused_computation.19.clone.1 | convolution fusion | flops 1762209792 | bytes 3772416 | tf_op jit(solution)/shard_map/while/body/eval_jaxpr/dot_general | solution.py:117
  118.0 2.2 %convolution_add_fusion.4 = f32[224,640]{1,0:T(8,128)S(1)} fusion(f32[224,640]{1,0:T(8,128)S(1)} %get-tuple-element.545, f32[1024,640]{0,1:T(8,128)S(1)} %bitcast.147, s32[1024]{0:T(1024)S(1)} %get-tuple-element.504), kind=kOutput, calls=%fused_computation.19.clone.1 | convolution fusion | flops 1762209792 | bytes 3772416 | tf_op jit(solution)/shard_map/while/body/eval_jaxpr/dot_general | solution.py:117
  120.7 2.2 %convolution_add_fusion.4 = f32[224,640]{1,0:T(8,128)S(1)} fusion(f32[224,640]{1,0:T(8,128)S(1)} %get-tuple-element.545, f32[1024,640]{0,1:T(8,128)S(1)} %bitcast.147, s32[1024]{0:T(1024)S(1)} %get-tuple-element.504), kind=kOutput, calls=%fused_computation.19.clone.1 | convolution fusion | flops 1762209792 | bytes 3772416 | tf_op jit(solution)/shard_map/while/body/eval_jaxpr/dot_general | solution.py:117
  123.3 2.2 %convolution_add_fusion.4 = f32[224,640]{1,0:T(8,128)S(1)} fusion(f32[224,640]{1,0:T(8,128)S(1)} %get-tuple-element.545, f32[1024,640]{0,1:T(8,128)S(1)} %bitcast.147, s32[1024]{0:T(1024)S(1)} %get-tuple-element.504), kind=kOutput, calls=%fused_computation.19.clone.1 | convolution fusion | flops 1762209792 | bytes 3772416 | tf_op jit(solution)/shard_map/while/body/eval_jaxpr/dot_general | solution.py:117
  125.6 5.4 %while.54 = (s32[]{:T(128)}, f32[224,640]{1,0:T(8,128)S(1)}, s32[2,1024]{1,0:T(2,128)S(1)}, f32[2,5,1024]{2,1,0:T(8,128)S(1)}, s32[]{:T(128)}) while((s32[]{:T(128)}, f32[224,640]{1,0:T(8,128)S(1)}, s32[2,1024]{1,0:T(2,128)S(1)}, f32[2,5,1024]{2,1,0:T(8,128)S(1)}, s32[]{:T(128)}) %tuple.159), condition=%wide.region_9.10_spmd, body=%wide.region_8.9_spmd.sunk | while | flops 1763146752 | bytes 7528517 | solution.py:122
  126.0 2.2 %convolution_add_fusion.5 = f32[224,640]{1,0:T(8,128)S(1)} fusion(f32[224,640]{1,0:T(8,128)S(1)} %get-tuple-element.578, f32[1024,640]{0,1:T(8,128)S(1)} %bitcast.148, s32[1024]{0:T(1024)S(1)} %get-tuple-element.517), kind=kOutput, calls=%fused_computation.54.clone.1 | convolution fusion | flops 1762209792 | bytes 3772416 | tf_op jit(solution)/shard_map/while/body/eval_jaxpr/dot_general | solution.py:117
  128.7 2.2 %convolution_add_fusion.5 = f32[224,640]{1,0:T(8,128)S(1)} fusion(f32[224,640]{1,0:T(8,128)S(1)} %get-tuple-element.578, f32[1024,640]{0,1:T(8,128)S(1)} %bitcast.148, s32[1024]{0:T(1024)S(1)} %get-tuple-element.517), kind=kOutput, calls=%fused_computation.54.clone.1 | convolution fusion | flops 1762209792 | bytes 3772416 | tf_op jit(solution)/shard_map/while/body/eval_jaxpr/dot_general | solution.py:117
  (158 shorter events, 23.5 us)
Async XLA Ops:
  7.2 4.6 %copy-start = (f32[1,1,3,64,512]{4,3,2,1,0:T(8,128)S(1)}, f32[1,1,3,64,512]{4,3,2,1,0:T(8,128)}, u32[]{:S(2)}) copy-start(f32[1,1,3,64,512]{4,3,2,1,0:T(8,128)} %param.26) | copy-start | bytes 1179652
  7.2 4.8 %copy-start.1 = (f32[1,1,64,512]{3,2,1,0:T(8,128)S(1)}, f32[1,1,64,512]{3,2,1,0:T(8,128)}, u32[]{:S(2)}) copy-start(f32[1,1,64,512]{3,2,1,0:T(8,128)} %param.25) | copy-start | bytes 393220
  7.2 103.2 %all-gather.3.cloned.1.call-start = ((), (), s32[]{:S(2)}) async-start(), calls=%async_computation | async-start | bytes 5406720 | tf_op jit(solution)/shard_map/all_gather | solution.py:169
  8.7 3.4 %copy-start.2 = (f32[512,512,1]{1,0,2:T(8,128)S(1)}, f32[512,512,1]{1,0,2:T(8,128)}, u32[]{:S(2)}) copy-start(f32[512,512,1]{1,0,2:T(8,128)} %constant.360) | copy-start | bytes 3145732
  10.9 2.3 %copy-start.4 = (f32[512,512,1]{1,0,2:T(8,128)S(1)}, f32[512,512,1]{1,0,2:T(8,128)}, u32[]{:S(2)}) copy-start(f32[512,512,1]{1,0,2:T(8,128)} %constant.361) | copy-start | bytes 3145732
  12.0 2.3 %copy-start.3 = (f32[512,512,1]{1,0,2:T(8,128)S(1)}, f32[512,512,1]{1,0,2:T(8,128)}, u32[]{:S(2)}) copy-start(f32[512,512,1]{1,0,2:T(8,128)} %constant.362) | copy-start | bytes 3145732
  14.3 1.3 copy-start.7
  16.3 0.8 copy-start.6
  16.4 0.8 copy-start.8
  17.1 24.9 %copy-start.5 = (s32[1,1,2,1024]{3,2,1,0:T(2,128)S(1)}, s32[1,1,2,1024]{3,2,1,0:T(2,128)}, u32[]{:S(2)}) copy-start(s32[1,1,2,1024]{3,2,1,0:T(2,128)} %param.30) | copy-start | bytes 24580
  17.2 24.9 %copy-start.9 = (s32[1,1,2]{2,1,0:T(1,128)S(1)}, s32[1,1,2]{2,1,0:T(1,128)}, u32[]{:S(2)}) copy-start(s32[1,1,2]{2,1,0:T(1,128)} %param.31) | copy-start | bytes 28
  48.4 14.1 %collective-permute-start = (f32[5,1,1024]{2,0,1:T(8,128)S(1)}, f32[5,1,1024]{2,0,1:T(8,128)S(1)}, u32[]{:S(2)}, u32[]{:S(2)}) collective-permute-start(f32[5,1,1024]{2,0,1:T(8,128)S(1)} %get-tuple-element.381), channel_id=1, source_target_pairs={{0,32},{32,64},{64,96},{96,128},{128,160},{160,192},{192,224},{224... | collective-permute-start | bytes 61448 | tf_op jit(solution)/shard_map/ppermute | solution.py:19
  52.8 10.5 %collective-permute-start.1 = (f32[5,1,1024]{2,0,1:T(8,128)S(1)}, f32[5,1,1024]{2,0,1:T(8,128)S(1)}, u32[]{:S(2)}, u32[]{:S(2)}) collective-permute-start(f32[5,1,1024]{2,0,1:T(8,128)S(1)} %get-tuple-element.382), channel_id=1, source_target_pairs={{32,0},{64,32},{96,64},{128,96},{160,128},{192,160},{224,192},{256... | collective-permute-start | bytes 61448 | tf_op jit(solution)/shard_map/ppermute | solution.py:21
Sparse Core Ops, SparseCore 0:
  42.1 68.2 all-gather.2
where the time goes:
time: 141 us
  waiting for transfers between devices  47.9 us (34%)
  matrix products  29 us (21%)
  local copies, waits for them, and re-layouts  18.1 us (13%)
  other arithmetic  16.4 us (12%)
  between operations  14.6 us (10%)
  starting transfers between devices  14.1 us (10%)
    all_gather x1, waiting for transfers between devices, local(): gathered = lax.all_gather(section_send[None], 'cube', axis=0, tiled=True)  47.1 us
    dot_general x7, matrix products, add_one_row(): lax.dot_general(high_part, spread, (((0,), (0,)), ((), ())), precision=la...  15.6 us
    dot_general x7, matrix products, pick_one_row(): jnp.dot(high_part, flat_table, precision=lax.Precision.HIGHEST)  10.1 us
    ppermute x1, starting transfers between devices, with_halo(): lax.ppermute(head, axis, [((i + 1) % count, i) for i in range(count)])  9.68 us
    dynamic_update_slice x10, local copies, waits for them, and re-layouts, pick_rows(): return jnp.moveaxis(lax.map(pick_one_row, (slot_ids, counts)), 0, 1)  8.4 us
    convert_element_type x7, other arithmetic, pick_one_row(): live_mask = (jnp.arange(row_ids.shape[0]) < count).astype(jnp.float32)  4.62 us
    dynamic_slice x21, local copies, waits for them, and re-layouts, pick_rows(): return jnp.moveaxis(lax.map(pick_one_row, (slot_ids, counts)), 0, 1)  4.58 us
    ppermute x1, starting transfers between devices, with_halo(): lax.ppermute(tail, axis, [(i, (i + 1) % count) for i in range(count)])  4.35 us
  transfers between devices with their start and end apart: 3, of which 2 were waited for; matrix products, arithmetic and copies ran while one was open for 4% of the time, Pallas kernels for 0%

commit v1 on v0

--- a/solution.py
+++ b/solution.py
@@ -166,7 +166,10 @@
     cross_send = pick_rows(table, cross_ids, cross_counts[0, 0])
     sections = lax.axis_size("cube").bit_length() - 1
     received = []
-    gathered = lax.all_gather(section_send[None], "cube", axis=0, tiled=True)
+    gathered = jnp.concatenate(
+        lax.all_to_all(jnp.stack([section_send[None]] * lax.axis_size("cube")), "cube", 0, 0),
+        axis=0,
+    )
     position = lax.axis_index("cube")
     for b in range(sections):
         partner = jnp.bitwise_xor(position, 1 << b)

time: 141 us -> 106 us (0.75)
  waiting for transfers between devices: 47.9 us -> 23.8 us
  between operations: 14.6 us -> 1.2 us
  starting transfers between devices: 14.1 us -> 22 us
  local copies, waits for them, and re-layouts: 18.1 us -> 12.9 us
    all_gather x1 -> x0, waiting for transfers between devices: 47.1 us -> none  [local(): gathered = lax.all_gather(section_send[None], 'cube', axis=0, tiled=True)]
    all_to_all x0 -> x1, waiting for transfers between devices: none -> 23 us  [local(): lax.all_to_all(jnp.stack([section_send[None]] * lax.axis_size('cube')), '...]
    all_to_all x0 -> x1, starting transfers between devices: none -> 11.4 us  [local(): lax.all_to_all(jnp.stack([section_send[None]] * lax.axis_size('cube')), '...]
    dynamic_update_slice x10 -> x0, local copies, waits for them, and re-layouts: 8.4 us -> none  [pick_rows(): return jnp.moveaxis(lax.map(pick_one_row, (slot_ids, counts)), 0, 1)]
    another operation x0 -> x1, local copies, waits for them, and re-layouts: none -> 3.41 us  [local(): jnp.stack([section_send[None]] * lax.axis_size('cube'))]
    ppermute x1, starting transfers between devices: 4.35 us -> 1.92 us  [with_halo(): lax.ppermute(tail, axis, [(i, (i + 1) % count) for i in range(count)])]
  transfers between devices with their start and end apart: 3 -> 3, of which waited for: 2 -> 2; matrix products, arithmetic and copies ran while one was open for 4% -> 6% of each run, Pallas kernels for 0% -> 0%
where the time goes in v1:
time: 106 us
  matrix products  29.1 us (27%)
  waiting for transfers between devices  23.8 us (22%)
  starting transfers between devices  22 us (21%)
  other arithmetic  15.9 us (15%)
  local copies, waits for them, and re-layouts  12.9 us (12%)
  between operations  1.2 us (1%)
    all_to_all x1, waiting for transfers between devices, local(): lax.all_to_all(jnp.stack([section_send[None]] * lax.axis_size('cube')), '...  23 us
    dot_general x7, matrix products, add_one_row(): lax.dot_general(high_part, spread, (((0,), (0,)), ((), ())), precision=la...  15.7 us
    all_to_all x1, starting transfers between devices, local(): lax.all_to_all(jnp.stack([section_send[None]] * lax.axis_size('cube')), '...  11.4 us
    dot_general x7, matrix products, pick_one_row(): jnp.dot(high_part, flat_table, precision=lax.Precision.HIGHEST)  10.2 us
    ppermute x1, starting transfers between devices, with_halo(): lax.ppermute(head, axis, [((i + 1) % count, i) for i in range(count)])  8.67 us
    dynamic_slice x21, local copies, waits for them, and re-layouts, pick_rows(): return jnp.moveaxis(lax.map(pick_one_row, (slot_ids, counts)), 0, 1)  4.39 us
    convert_element_type x7, other arithmetic, pick_one_row(): live_mask = (jnp.arange(row_ids.shape[0]) < count).astype(jnp.float32)  4.1 us
    another operation x1, local copies, waits for them, and re-layouts, local(): jnp.stack([section_send[None]] * lax.axis_size('cube'))  3.41 us
  transfers between devices with their start and end apart: 3, of which 2 were waited for; matrix products, arithmetic and copies ran while one was open for 6% of the time, Pallas kernels for 0%

profile of v1, /device:TPU:1, one launch (start us, length us, event | category | flops | bytes accessed | tf_op | source)
XLA Modules:
  0.0 105.9 jit_solution(17025882488996564671)
XLA Ops:
  2.1 1.1 %slice_bitcast_fusion.5 = (f32[1,64,512]{2,1,0:T(8,128)S(1)}, f32[1,64,512]{2,1,0:T(8,128)S(1)}, f32[1,64,512]{2,1,0:T(8,128)S(1)}) fusion(f32[1,1,3,64,512]{4,3,2,1,0:T(8,128)} %param.26), kind=kLoop, calls=%fused_computation.119 | loop fusion | bytes 786432 | tf_op jit(solution)/shard_map/slice | solution.py:146
  3.2 1.1 %bitcast_divide_fusion = f32[3,64,512]{2,1,0:T(8,128)S(1)} fusion(f32[1,1,3,64,512]{4,3,2,1,0:T(8,128)} %param.26, f32[64,512]{1,0:T(8,128)} %bitcast.156), kind=kLoop, calls=%fused_computation.93 | loop fusion | flops 98304 | bytes 917504 | tf_op jit(solution)/shard_map/div | solution.py:138
  4.4 0.8 broadcast_multiply_fusion.3
  5.5 1.1 %convolution_subtract_fusion.2 = f32[4,64,512]{2,1,0:T(8,128)S(1)} fusion(f32[512,512,1]{1,0,2:T(8,128)S(1)} %copy-done.2, f32[3,64,512]{2,1,0:T(8,128)S(1)} %get-tuple-element.394, f32[1,64,512]{2,1,0:T(8,128)S(1)} %get-tuple-element.385, f32[64]{0:T(128)S(1)} %get-tuple-element.399), kind=kOutput, calls=%fused_computation.76 | convolution fusion | flops 805699584 | bytes 2097408 | tf_op jit(solution)/shard_map/dot_general | solution.py:149
  6.6 1.1 %convolution_subtract_fusion.1 = f32[4,64,512]{2,1,0:T(8,128)S(1)} fusion(f32[4,64,512]{2,1,0:T(8,128)S(1)} %convolution_subtract_fusion.2, f32[512,512,1]{1,0,2:T(8,128)S(1)} %copy-done.4, f32[3,64,512]{2,1,0:T(8,128)S(1)} %get-tuple-element.393, f32[1,64,512]{2,1,0:T(8,128)S(1)} %get-tuple-element.384, f32[64]{0:T(128)S(1)} %get-tuple-element.398), kind=kOutput, calls=%fused_computation.75 | convolution fusion | flops 805699584 | bytes 2621696 | tf_op jit(solution)/shard_map/dot_general | solution.py:149
  7.8 1.1 %fusion.25 = f32[4,64,512]{2,1,0:T(8,128)S(1)} fusion(f32[4,64,512]{2,1,0:T(8,128)S(1)} %convolution_subtract_fusion.1, f32[512,512,1]{1,0,2:T(8,128)S(1)} %copy-done.3, f32[3,64,512]{2,1,0:T(8,128)S(1)} %get-tuple-element.392, f32[1,64,512]{2,1,0:T(8,128)S(1)} %get-tuple-element.383, f32[64,512]{1,0:T(8,128)S(1)} %broadcast_multiply_fusion.3, ...), kind=kOutput, calls=%fused_computation.77 | convolution fusion | flops 805830656 | bytes 2752768 | tf_op jit(solution)/shard_map/dot_general | solution.py:149
  10.6 15.7 %while.51 = (s32[]{:T(128)}, f32[5,5,1024]{2,1,0:T(8,128)S(1)}, s32[5,1024]{1,0:T(8,128)S(1)}, f32[224,640]{1,0:T(8,128)S(1)}, s32[5]{0:T(128)S(1)}, /*index=5*/s32[]{:T(128)}) while((s32[]{:T(128)}, f32[5,5,1024]{2,1,0:T(8,128)S(1)}, s32[5,1024]{1,0:T(8,128)S(1)}, f32[224,640]{1,0:T(8,128)S(1)}, s32[5]{0:T(128)S(1)}, ...), condition=%wide.region_2.0_spmd, body=%wide.region_0.2_spmd.sunk | while | flops 1763431424 | bytes 6987869 | solution.py:107
  10.6 1.5 %fusion.65 = f32[1024,640]{0,1:T(8,128)S(1)} fusion(f32[224,640]{1,0:T(8,128)S(1)} %get-tuple-element.547, s32[1024]{0:T(1024)S(1)} %get-tuple-element.511), kind=kOutput, calls=%fused_computation.2.clone.1 | convolution fusion | flops 1761837056 | bytes 3198976 | tf_op jit(solution)/shard_map/while/body/eval_jaxpr/dot_general | solution.py:100
  13.8 1.5 %fusion.65 = f32[1024,640]{0,1:T(8,128)S(1)} fusion(f32[224,640]{1,0:T(8,128)S(1)} %get-tuple-element.547, s32[1024]{0:T(1024)S(1)} %get-tuple-element.511), kind=kOutput, calls=%fused_computation.2.clone.1 | convolution fusion | flops 1761837056 | bytes 3198976 | tf_op jit(solution)/shard_map/while/body/eval_jaxpr/dot_general | solution.py:100
  16.9 1.4 %fusion.65 = f32[1024,640]{0,1:T(8,128)S(1)} fusion(f32[224,640]{1,0:T(8,128)S(1)} %get-tuple-element.547, s32[1024]{0:T(1024)S(1)} %get-tuple-element.511), kind=kOutput, calls=%fused_computation.2.clone.1 | convolution fusion | flops 1761837056 | bytes 3198976 | tf_op jit(solution)/shard_map/while/body/eval_jaxpr/dot_general | solution.py:100
  20.1 1.5 %fusion.65 = f32[1024,640]{0,1:T(8,128)S(1)} fusion(f32[224,640]{1,0:T(8,128)S(1)} %get-tuple-element.547, s32[1024]{0:T(1024)S(1)} %get-tuple-element.511), kind=kOutput, calls=%fused_computation.2.clone.1 | convolution fusion | flops 1761837056 | bytes 3198976 | tf_op jit(solution)/shard_map/while/body/eval_jaxpr/dot_general | solution.py:100
  23.2 1.5 %fusion.65 = f32[1024,640]{0,1:T(8,128)S(1)} fusion(f32[224,640]{1,0:T(8,128)S(1)} %get-tuple-element.547, s32[1024]{0:T(1024)S(1)} %get-tuple-element.511), kind=kOutput, calls=%fused_computation.2.clone.1 | convolution fusion | flops 1761837056 | bytes 3198976 | tf_op jit(solution)/shard_map/while/body/eval_jaxpr/dot_general | solution.py:100
  26.4 3.4 %stack.9 = f32[32,1,5,5,1024]{4,1,3,2,0:T(1,128)} broadcast(f32[5,5,1024]{2,1,0:T(8,128)S(1)} %copy.40), dimensions={2,3,4} | broadcast | bytes 3379200 | tf_op jit(solution)/shard_map/stack | solution.py:170
  29.8 11.4 %all-to-all-start = ((f32[32,1,5,5,1024]{4,1,3,2,0:T(1,128)}), f32[32,1,5,5,1024]{4,1,3,2,0:T(1,128)}, u32[]{:S(2)}, u32[]{:S(2)}) async-start(f32[32,1,5,5,1024]{4,1,3,2,0:T(1,128)} %stack.9), calls=%async_computation | async-start | bytes 6553600 | tf_op jit(solution)/shard_map/all_to_all | solution.py:170
  41.2 6.5 %while.53 = (s32[]{:T(128)}, f32[2,5,1024]{2,1,0:T(8,128)S(1)}, s32[2,1024]{1,0:T(2,128)S(1)}, f32[224,640]{1,0:T(8,128)S(1)}, s32[2]{0:T(128)S(1)}, /*index=5*/s32[]{:T(128)}) while((s32[]{:T(128)}, f32[2,5,1024]{2,1,0:T(8,128)S(1)}, s32[2,1024]{1,0:T(2,128)S(1)}, f32[224,640]{1,0:T(8,128)S(1)}, s32[2]{0:T(128)S(1)}, ...), condition=%wide.region_7.8_spmd, body=%wide.region_5.7_spmd.sunk | while | flops 1763431424 | bytes 6987869 | solution.py:107
  41.3 1.5 %fusion.72 = f32[1024,640]{0,1:T(8,128)S(1)} fusion(f32[224,640]{1,0:T(8,128)S(1)} %get-tuple-element.580, s32[1024]{0:T(1024)S(1)} %get-tuple-element.524), kind=kOutput, calls=%fused_computation.38.clone.1 | convolution fusion | flops 1761837056 | bytes 3198976 | tf_op jit(solution)/shard_map/while/body/eval_jaxpr/dot_general | solution.py:100
  44.5 1.5 %fusion.72 = f32[1024,640]{0,1:T(8,128)S(1)} fusion(f32[224,640]{1,0:T(8,128)S(1)} %get-tuple-element.580, s32[1024]{0:T(1024)S(1)} %get-tuple-element.524), kind=kOutput, calls=%fused_computation.38.clone.1 | convolution fusion | flops 1761837056 | bytes 3198976 | tf_op jit(solution)/shard_map/while/body/eval_jaxpr/dot_general | solution.py:100
  47.7 1.9 %collective-permute-start = (f32[5,1,1024]{2,0,1:T(8,128)S(1)}, f32[5,1,1024]{2,0,1:T(8,128)S(1)}, u32[]{:S(2)}, u32[]{:S(2)}) collective-permute-start(f32[5,1,1024]{2,0,1:T(8,128)S(1)} %get-tuple-element.395), channel_id=1, source_target_pairs={{0,32},{32,64},{64,96},{96,128},{128,160},{160,192},{192,224},{224... | collective-permute-start | bytes 61448 | tf_op jit(solution)/shard_map/ppermute | solution.py:19
  49.7 8.7 %collective-permute-start.1 = (f32[5,1,1024]{2,0,1:T(8,128)S(1)}, f32[5,1,1024]{2,0,1:T(8,128)S(1)}, u32[]{:S(2)}, u32[]{:S(2)}) collective-permute-start(f32[5,1,1024]{2,0,1:T(8,128)S(1)} %get-tuple-element.396), channel_id=1, source_target_pairs={{32,0},{64,32},{96,64},{128,96},{160,128},{192,160},{224,192},{256... | collective-permute-start | bytes 61448 | tf_op jit(solution)/shard_map/ppermute | solution.py:21
  58.4 0.8 collective-permute-done.1
  59.2 23.0 %all-to-all-done = f32[32,1,5,5,1024]{4,1,3,2,0:T(1,128)} async-done(((f32[32,1,5,5,1024]{4,1,3,2,0:T(1,128)}), f32[32,1,5,5,1024]{4,1,3,2,0:T(1,128)}, u32[]{:S(2)}, u32[]{:S(2)}) %all-to-all-start) | async-done | bytes 3276832 | tf_op jit(solution)/shard_map/all_to_all | solution.py:170
  82.1 1.1 %constant_dynamic-slice_fusion.5 = (f32[1,1,5,5,1024]{4,1,3,2,0:T(1,128)S(1)}, f32[1,1,5,5,1024]{4,1,3,2,0:T(1,128)S(1)}, f32[1,1,5,5,1024]{4,1,3,2,0:T(1,128)S(...) fusion(f32[32,1,5,5,1024]{4,1,3,2,0:T(1,128)} %all-to-all-done, s32[]{:T(128)S(6)} %select_n.125, ...), kind=kLoop, calls=%fused_computation.127 | loop fusion | bytes 1024020 | tf_op jit(solution)/shard_map/jit(dynamic_index_in_dim)/dynamic_slice | solution.py:176
  83.8 13.6 %while.52 = (s32[]{:T(128)}, f32[224,640]{1,0:T(8,128)S(1)}, s32[5,1024]{1,0:T(8,128)S(1)}, f32[5,5,1024]{2,0,1:T(8,128)S(1)}, s32[]{:T(128)}) while((s32[]{:T(128)}, f32[224,640]{1,0:T(8,128)S(1)}, s32[5,1024]{1,0:T(8,128)S(1)}, f32[5,5,1024]{2,0,1:T(8,128)S(1)}, s32[]{:T(128)}) %tuple.162), condition=%wide.region_4.5_spmd, body=%wide.region_3.4_spmd.sunk | while | flops 1763146752 | bytes 7569477 | solution.py:122
  84.3 2.2 %convolution_add_fusion.4 = f32[224,640]{1,0:T(8,128)S(1)} fusion(f32[224,640]{1,0:T(8,128)S(1)} %get-tuple-element.556, f32[1024,640]{0,1:T(8,128)S(1)} %bitcast.147, s32[1024]{0:T(1024)S(1)} %get-tuple-element.518), kind=kOutput, calls=%fused_computation.19.clone.1 | convolution fusion | flops 1762209792 | bytes 3772416 | tf_op jit(solution)/shard_map/while/body/eval_jaxpr/dot_general | solution.py:117
  87.0 2.2 %convolution_add_fusion.4 = f32[224,640]{1,0:T(8,128)S(1)} fusion(f32[224,640]{1,0:T(8,128)S(1)} %get-tuple-element.556, f32[1024,640]{0,1:T(8,128)S(1)} %bitcast.147, s32[1024]{0:T(1024)S(1)} %get-tuple-element.518), kind=kOutput, calls=%fused_computation.19.clone.1 | convolution fusion | flops 1762209792 | bytes 3772416 | tf_op jit(solution)/shard_map/while/body/eval_jaxpr/dot_general | solution.py:117
  89.7 2.2 %convolution_add_fusion.4 = f32[224,640]{1,0:T(8,128)S(1)} fusion(f32[224,640]{1,0:T(8,128)S(1)} %get-tuple-element.556, f32[1024,640]{0,1:T(8,128)S(1)} %bitcast.147, s32[1024]{0:T(1024)S(1)} %get-tuple-element.518), kind=kOutput, calls=%fused_computation.19.clone.1 | convolution fusion | flops 1762209792 | bytes 3772416 | tf_op jit(solution)/shard_map/while/body/eval_jaxpr/dot_general | solution.py:117
  92.4 2.2 %convolution_add_fusion.4 = f32[224,640]{1,0:T(8,128)S(1)} fusion(f32[224,640]{1,0:T(8,128)S(1)} %get-tuple-element.556, f32[1024,640]{0,1:T(8,128)S(1)} %bitcast.147, s32[1024]{0:T(1024)S(1)} %get-tuple-element.518), kind=kOutput, calls=%fused_computation.19.clone.1 | convolution fusion | flops 1762209792 | bytes 3772416 | tf_op jit(solution)/shard_map/while/body/eval_jaxpr/dot_general | solution.py:117
  95.1 2.2 %convolution_add_fusion.4 = f32[224,640]{1,0:T(8,128)S(1)} fusion(f32[224,640]{1,0:T(8,128)S(1)} %get-tuple-element.556, f32[1024,640]{0,1:T(8,128)S(1)} %bitcast.147, s32[1024]{0:T(1024)S(1)} %get-tuple-element.518), kind=kOutput, calls=%fused_computation.19.clone.1 | convolution fusion | flops 1762209792 | bytes 3772416 | tf_op jit(solution)/shard_map/while/body/eval_jaxpr/dot_general | solution.py:117
  97.4 5.4 %while.54 = (s32[]{:T(128)}, f32[224,640]{1,0:T(8,128)S(1)}, s32[2,1024]{1,0:T(2,128)S(1)}, f32[2,5,1024]{2,1,0:T(8,128)S(1)}, s32[]{:T(128)}) while((s32[]{:T(128)}, f32[224,640]{1,0:T(8,128)S(1)}, s32[2,1024]{1,0:T(2,128)S(1)}, f32[2,5,1024]{2,1,0:T(8,128)S(1)}, s32[]{:T(128)}) %tuple.160), condition=%wide.region_9.10_spmd, body=%wide.region_8.9_spmd.sunk | while | flops 1763146752 | bytes 7528517 | solution.py:122
  97.8 2.2 %convolution_add_fusion.5 = f32[224,640]{1,0:T(8,128)S(1)} fusion(f32[224,640]{1,0:T(8,128)S(1)} %get-tuple-element.589, f32[1024,640]{0,1:T(8,128)S(1)} %bitcast.148, s32[1024]{0:T(1024)S(1)} %get-tuple-element.531), kind=kOutput, calls=%fused_computation.55.clone.1 | convolution fusion | flops 1762209792 | bytes 3772416 | tf_op jit(solution)/shard_map/while/body/eval_jaxpr/dot_general | solution.py:117
  100.5 2.2 %convolution_add_fusion.5 = f32[224,640]{1,0:T(8,128)S(1)} fusion(f32[224,640]{1,0:T(8,128)S(1)} %get-tuple-element.589, f32[1024,640]{0,1:T(8,128)S(1)} %bitcast.148, s32[1024]{0:T(1024)S(1)} %get-tuple-element.531), kind=kOutput, calls=%fused_computation.55.clone.1 | convolution fusion | flops 1762209792 | bytes 3772416 | tf_op jit(solution)/shard_map/while/body/eval_jaxpr/dot_general | solution.py:117
  104.3 0.8 add.181
  (155 shorter events, 20.5 us)
Async XLA Ops:
  0.6 4.6 %copy-start = (f32[1,1,3,64,512]{4,3,2,1,0:T(8,128)S(1)}, f32[1,1,3,64,512]{4,3,2,1,0:T(8,128)}, u32[]{:S(2)}) copy-start(f32[1,1,3,64,512]{4,3,2,1,0:T(8,128)} %param.26) | copy-start | bytes 1179652
  0.6 4.8 %copy-start.1 = (f32[1,1,64,512]{3,2,1,0:T(8,128)S(1)}, f32[1,1,64,512]{3,2,1,0:T(8,128)}, u32[]{:S(2)}) copy-start(f32[1,1,64,512]{3,2,1,0:T(8,128)} %param.25) | copy-start | bytes 393220
  2.1 3.4 %copy-start.2 = (f32[512,512,1]{1,0,2:T(8,128)S(1)}, f32[512,512,1]{1,0,2:T(8,128)}, u32[]{:S(2)}) copy-start(f32[512,512,1]{1,0,2:T(8,128)} %constant.365) | copy-start | bytes 3145732
  4.4 2.3 %copy-start.4 = (f32[512,512,1]{1,0,2:T(8,128)S(1)}, f32[512,512,1]{1,0,2:T(8,128)}, u32[]{:S(2)}) copy-start(f32[512,512,1]{1,0,2:T(8,128)} %constant.366) | copy-start | bytes 3145732
  5.4 2.3 %copy-start.3 = (f32[512,512,1]{1,0,2:T(8,128)S(1)}, f32[512,512,1]{1,0,2:T(8,128)}, u32[]{:S(2)}) copy-start(f32[512,512,1]{1,0,2:T(8,128)} %constant.367) | copy-start | bytes 3145732
  7.7 1.3 %copy-start.7 = (f32[8,64]{1,0:T(8,128)S(1)}, f32[8,64]{1,0:T(8,128)}, u32[]{:S(2)}) copy-start(f32[8,64]{1,0:T(8,128)} %constant.364) | copy-start | bytes 6148
  9.8 0.8 copy-start.6
  9.8 0.8 copy-start.8
  29.8 11.4 %copy-start.5 = (s32[1,1,2,1024]{3,2,1,0:T(2,128)S(1)}, s32[1,1,2,1024]{3,2,1,0:T(2,128)}, u32[]{:S(2)}) copy-start(s32[1,1,2,1024]{3,2,1,0:T(2,128)} %param.30) | copy-start | bytes 24580
  29.8 11.4 %copy-start.9 = (s32[1,1,2]{2,1,0:T(1,128)S(1)}, s32[1,1,2]{2,1,0:T(1,128)}, u32[]{:S(2)}) copy-start(s32[1,1,2]{2,1,0:T(1,128)} %param.31) | copy-start | bytes 28
  29.8 52.4 %all-to-all-start = ((f32[32,1,5,5,1024]{4,1,3,2,0:T(1,128)}), f32[32,1,5,5,1024]{4,1,3,2,0:T(1,128)}, u32[]{:S(2)}, u32[]{:S(2)}) async-start(f32[32,1,5,5,1024]{4,1,3,2,0:T(1,128)} %stack.9), calls=%async_computation | async-start | bytes 6553600 | tf_op jit(solution)/shard_map/all_to_all | solution.py:170
  47.7 10.6 %collective-permute-start = (f32[5,1,1024]{2,0,1:T(8,128)S(1)}, f32[5,1,1024]{2,0,1:T(8,128)S(1)}, u32[]{:S(2)}, u32[]{:S(2)}) collective-permute-start(f32[5,1,1024]{2,0,1:T(8,128)S(1)} %get-tuple-element.395), channel_id=1, source_target_pairs={{0,32},{32,64},{64,96},{96,128},{128,160},{160,192},{192,224},{224... | collective-permute-start | bytes 61448 | tf_op jit(solution)/shard_map/ppermute | solution.py:19
  49.7 9.5 %collective-permute-start.1 = (f32[5,1,1024]{2,0,1:T(8,128)S(1)}, f32[5,1,1024]{2,0,1:T(8,128)S(1)}, u32[]{:S(2)}, u32[]{:S(2)}) collective-permute-start(f32[5,1,1024]{2,0,1:T(8,128)S(1)} %get-tuple-element.396), channel_id=1, source_target_pairs={{32,0},{64,32},{96,64},{128,96},{160,128},{192,160},{224,192},{256... | collective-permute-start | bytes 61448 | tf_op jit(solution)/shard_map/ppermute | solution.py:21
